TPU v7x, 512 devices: a whole 4x4x16 slice. The times are simulated.
512 devices in a mesh: dp: 8 (over y, core), expert: 64 (over x, z).
Axes of the slice: x: 4, y: 4, z: 16, core: 2. Of those that a mesh axis runs over, the one named last changes fastest.
Arguments:
- grad_out: bfloat16 [32768, 4096], P('expert', 'dp'), may hold values from -30 to 30
- hidden: bfloat16 [32768, 2, 1024], P('expert', None, 'dp'), may hold values from -24 to 24
- gate_prob: float32 [32768, 2], P('expert'), may hold values from 0.05 to 1
- expert_ids: int32 [32768, 2], P('expert'), may hold values from 0 to 63, all different within a row; in each aligned block of 512 rows (0 to 511, 512 to 1023, ...) at most 20 rows name the same one
- weights: bfloat16 [64, 1024, 4096], P('expert', None, 'dp'), may hold values from -0.1875 to 0.1875
Outputs:
- hidden_grad: bfloat16 [32768, 2, 1024], P('expert', None, 'dp')
- update: float32 [64, 1024, 4096], P('expert', None, 'dp')
Inputs may be any that keep to these rules, and one draw needn't show every extreme that they name: `expert_ids`: among the 512 tokens of one index of expert, no expert is named by more than 20 choices, a bound that some block reaches; the 2 experts of a token differ.
All inputs are finite; a program needn't handle non-finite values.
Results may differ from a plain program's by a relative error of at most 0.019.
Values may be sent and summed in bfloat16 or wider, within the bound.
No kernel may reach another device: no remote copies, remote signals or barrier semaphores. Data moves between devices by JAX's collectives and lax.ppermute only.
A program may use at most 64 MiB of HBM per device.

v0:
```python
import jax
import jax.numpy as jnp
from jax import lax
from jax.sharding import PartitionSpec as P

D = 4096


def slot_numbers(route_ids, capacity, expert_count):
    flat_ids = route_ids.reshape(-1)
    one_hot = (flat_ids[:, None] == jnp.arange(expert_count, dtype=jnp.int32)[None, :]).astype(
        jnp.int32
    )
    before = jnp.cumsum(one_hot, axis=0) - one_hot
    rank_in = jnp.sum(before * one_hot, axis=1)
    return flat_ids * capacity + rank_in


def gram_sum(matrix_part):
    partial_gram = jnp.dot(matrix_part, matrix_part.T, preferred_element_type=jnp.float32)
    return lax.psum(partial_gram.astype(jnp.bfloat16), "dp").astype(jnp.float32)


def place_slots(slot_index, values, slot_count):
    empty_rows = jnp.zeros((slot_count,) + values.shape[1:], values.dtype)
    return empty_rows.at[slot_index].set(values)


def per_device(grad_out, hidden, gate_prob, expert_ids, weights):
    tokens, width_part = grad_out.shape
    top_count = expert_ids.shape[1]
    experts = lax.axis_size("expert")
    capacity = 5 * tokens * top_count // (4 * experts)
    total_slots = experts * capacity
    pair_count = tokens * top_count
    slot_index = slot_numbers(expert_ids, capacity, experts)
    token_of = jnp.arange(pair_count, dtype=jnp.int32) // top_count
    send_grad = place_slots(slot_index, grad_out[token_of], total_slots).reshape(
        experts, capacity, width_part
    )
    scaled_part = (gate_prob[:, :, None] * hidden.astype(jnp.float32)).astype(jnp.bfloat16)
    whole_scaled = lax.all_gather(scaled_part, "dp", axis=2, tiled=True)
    send_scaled = place_slots(
        slot_index, whole_scaled.reshape(pair_count, -1), total_slots
    ).reshape(experts, capacity, -1)
    got_grad, got_scaled = (
        lax.all_to_all(send_grad, "expert", split_axis=0, concat_axis=0, tiled=True),
        lax.all_to_all(send_scaled, "expert", split_axis=0, concat_axis=0, tiled=True),
    )
    got_grad = got_grad.reshape(total_slots, width_part)
    got_scaled = got_scaled.reshape(total_slots, -1)
    weight_part = weights[0]
    gradient = lax.dot_general(
        got_scaled, got_grad, (((0,), (0,)), ((), ())), preferred_element_type=jnp.float32
    )
    back_term = lax.dot_general(
        got_grad, weight_part, (((1,), (1,)), ((), ())), preferred_element_type=jnp.float32
    )
    flat_prob = gate_prob.reshape(-1)
    summed = lax.psum_scatter(
        back_term.astype(jnp.bfloat16), "dp", scatter_dimension=1, tiled=True
    ).astype(jnp.float32)
    returned = lax.all_to_all(
        summed.reshape(experts, capacity, -1).astype(jnp.bfloat16),
        "expert",
        split_axis=0,
        concat_axis=0,
        tiled=True,
    ).astype(jnp.float32)
    picked = returned.reshape(total_slots, -1)[slot_index]
    hidden_grad = (flat_prob[:, None] * picked).astype(jnp.bfloat16).reshape(tokens, top_count, -1)
    grad_bf16 = gradient.astype(jnp.bfloat16)
    gram_first = gram_sum(grad_bf16)
    norm_sq = jnp.sqrt(jnp.sum(gram_first * gram_first)) + 1e-06
    current = (grad_bf16.astype(jnp.float32) * lax.rsqrt(norm_sq)).astype(jnp.bfloat16)
    gram_now = (gram_first / norm_sq).astype(jnp.bfloat16)
    following = current.astype(jnp.float32)
    for sweep_number in range(2):
        if sweep_number > 0:
            gram_now = gram_sum(current).astype(jnp.bfloat16)
        following = 1.5 * current.astype(jnp.float32) - 0.5 * jnp.dot(
            gram_now, current, preferred_element_type=jnp.float32
        )
        current = following.astype(jnp.bfloat16)
    update = following * D**0.5
    return (hidden_grad, update[None])


def solution(mesh):
    in_specs = (
        P("expert", "dp"),
        P("expert", None, "dp"),
        P("expert", None),
        P("expert", None),
        P("expert", None, "dp"),
    )
    out_specs = (P("expert", None, "dp"), P("expert", None, "dp"))
    return jax.shard_map(
        per_device, mesh=mesh, in_specs=in_specs, out_specs=out_specs, check_vma=False
    )
```

profile of v0, /device:TPU:2, one launch (start us, length us, event | category | flops | bytes accessed | tf_op | source)
XLA Modules:
  0.0 626.0 jit_solution(6197987789082699378)
XLA Ops:
  7.2 0.0 copy-start
  7.2 0.0 reduce-scatter.4.cloned.1.call-start
  7.2 0.8 broadcast_multiply_fusion
  8.0 0.8 copy.19
  8.8 0.2 eq.29
  9.0 0.2 eq.25
  9.2 0.1 copy.18
  9.3 0.2 mul.64
  9.6 18.0 %reduce-window.6 = s32[64,8,128]{2,1,0:T(8,128)S(1)} reduce-window(s32[64,8,128]{2,1,0:T(8,128)S(1)} %fusion.21, s32[]{:T(128)} %constant.16.clone.1), window={size=1x1x128 pad=0_0x0_0x127_0}, to_apply=%region_0.0 | reduce-window | flops 8323072 | bytes 524292 | tf_op jit(solution)/shard_map/reduce-window
  27.6 0.1 slice.12
  27.7 0.1 copy.21
  27.9 0.1 copy.22
  28.0 0.1 broadcast_add_fusion
  28.1 0.1 fusion.20
  28.2 12.8 %scatter_custom_fusion = bf16[1280,512]{1,0:T(8,128)(2,1)S(1)} fusion(s32[1024]{0:T(1024)S(1)} %bitcast.46, bf16[512,512]{1,0:T(8,128)(2,1)} %param.5, s32[1024]{0:T(1024)S(1)} %broadcast_clamp_fusion.1, bf16[]{:T(256)} %constant.13.clone.1), kind=kCustom, calls=%fused_computation.22 | custom fusion | bytes 1311232 | tf_op jit(solution)/shard_map/scatter | solution.py:26
  41.0 1.3 reshape.124
  42.3 94.8 %all_to_all.15 = bf16[64,20,512]{2,1,0:T(8,128)(2,1)S(1)} all-to-all(bf16[64,20,512]{2,1,0:T(8,128)(2,1)} %reshape.124), channel_id=1, replica_groups=mesh['dp'=8,'expert'=64] {'expert'}, dimensions={0} | all-to-all | bytes 2621440 | tf_op jit(solution)/shard_map/all_to_all | solution.py:47
  137.1 1.2 reshape.125
  138.3 0.0 copy-done
  138.3 4.4 convolution_convert_fusion
  142.7 4.4 copy.25
  147.1 0.0 copy-start.2
  147.1 0.0 reduce-scatter.4.cloned.1.call-update
  147.1 35.3 %reduce-scatter.4.cloned.1.call-done = bf16[128,1280]{1,0:T(8,128)(2,1)} async-done(((bf16[1024,1280]{1,0:T(8,128)(2,1)}), bf16[128,1280]{1,0:T(8,128)(2,1)}) %reduce-scatter.4.cloned.1.call-update) | async-done | bytes 327696
  182.4 1.2 copy.26
  183.5 0.8 convert_element_type.61
  184.4 15.8 %all-to-all-start.1 = ((bf16[64,20,128]{2,1,0:T(8,128)(2,1)}), bf16[64,20,128]{2,1,0:T(8,128)(2,1)}, u32[]{:S(2)}, u32[]{:S(2)}) async-start(bf16[64,20,128]{2,1,0:T(8,128)(2,1)} %convert_element_type.61), calls=%async_computation.1 | async-start | bytes 786432 | tf_op jit(solution)/shard_map/all_to_all | solution.py:63
  200.2 0.0 all-gather.2.cloned.1.call-start
  200.3 0.0 copy-done.2
  200.3 0.1 copy.17
  200.4 23.1 %all-to-all-done.1 = bf16[64,20,128]{2,1,0:T(8,128)(2,1)} async-done(((bf16[64,20,128]{2,1,0:T(8,128)(2,1)}), bf16[64,20,128]{2,1,0:T(8,128)(2,1)}, u32[]{:S(2)}, u32[]{:S(2)}) %all-to-all-start.1) | async-done | bytes 327712 | tf_op jit(solution)/shard_map/all_to_all | solution.py:63
  223.6 1.1 reshape.131
  224.6 4.0 gather_fusion
  228.7 2.4 multiply_convert_fusion.2
  231.1 0.0 all-gather.2.cloned.1.call-update
  231.1 0.2 all-reduce.3.cloned.1.call-start
  231.4 35.5 %all-gather.2.cloned.1.call-done = bf16[512,2,1024]{2,1,0:T(2,128)(2,1)} async-done(((bf16[512,2,128]{2,1,0:T(2,128)(2,1)}), bf16[512,2,1024]{2,1,0:T(2,128)(2,1)}) %all-gather.2.cloned.1.call-update) | async-done | bytes 2097168 | tf_op jit(solution)/shard_map/all_gather | solution.py:42
  266.8 4.1 reshape.160
  270.9 7.8 %scatter_custom_fusion.1 = bf16[1280,1024]{1,0:T(8,128)(2,1)} fusion(s32[1024]{0:T(1024)S(1)} %bitcast.48, bf16[1024,1024]{1,0:T(8,128)(2,1)} %reshape.160, bf16[]{:T(256)} %constant.13.clone.1), kind=kCustom, calls=%fused_computation.19 | custom fusion | bytes 2621952 | tf_op jit(solution)/shard_map/scatter | solution.py:26
  278.7 5.2 reshape.129
  283.9 159.6 %all_to_all.16 = bf16[64,20,1024]{2,1,0:T(8,128)(2,1)S(1)} all-to-all(bf16[64,20,1024]{2,1,0:T(8,128)(2,1)} %reshape.129), channel_id=1, replica_groups=mesh['dp'=8,'expert'=64] {'expert'}, dimensions={0} | all-to-all | bytes 5242880 | tf_op jit(solution)/shard_map/all_to_all | solution.py:48
  443.5 2.9 bitcast_convert_fusion
  446.4 0.0 copy-start.3
  446.4 1.0 copy-done.3
  447.3 2.6 convolution_convert_fusion.2
  449.9 0.0 all-reduce.3.cloned.1.call-update
  450.0 0.3 all-reduce.5.cloned.1.call-start
  450.2 73.4 %all-reduce.3.cloned.1.call-done = bf16[1024,1024]{1,0:T(8,128)(2,1)} async-done(((bf16[1024,1024]{1,0:T(8,128)(2,1)}), bf16[1024,1024]{1,0:T(8,128)(2,1)}) %all-reduce.3.cloned.1.call-update) | async-done | bytes 2097168 | tf_op jit(solution)/shard_map/psum | solution.py:21
  523.6 0.0 copy-start.1
  523.6 3.4 fusion
  527.8 0.0 copy-done.1
  527.8 2.9 subtract_convert_fusion
  530.8 0.0 copy-start.4
  530.8 1.0 copy-done.4
  531.7 2.6 convolution_convert_fusion.1
  534.3 0.0 copy-start.5
  534.3 0.0 all-reduce.5.cloned.1.call-update
  534.4 80.9 %all-reduce.5.cloned.1.call-done = bf16[1024,1024]{1,0:T(8,128)(2,1)} async-done(((bf16[1024,1024]{1,0:T(8,128)(2,1)}), bf16[1024,1024]{1,0:T(8,128)(2,1)}) %all-reduce.5.cloned.1.call-update) | async-done | bytes 2097168 | tf_op jit(solution)/shard_map/psum | solution.py:21
  615.2 0.0 copy-done.5
  615.2 4.2 multiply_bitcast_fusion
  (7 shorter events, 0.1 us)
Async XLA Ops:
  7.2 131.1 %copy-start = (bf16[1,1024,512]{2,1,0:T(8,128)(2,1)S(1)}, bf16[1,1024,512]{2,1,0:T(8,128)(2,1)}, u32[]{:S(2)}) copy-start(bf16[1,1024,512]{2,1,0:T(8,128)(2,1)} %param.9) | copy-start | bytes 3145732
  7.2 175.2 %reduce-scatter.4.cloned.1.call-start = ((), (), s32[]{:S(2)}) async-start(), calls=%async_computation.7 | async-start | bytes 2949120
  147.1 53.2 %copy-start.2 = (f32[512,2]{0,1:T(2,128)S(1)}, f32[512,2]{0,1:T(2,128)}, u32[]{:S(2)}) copy-start(f32[512,2]{0,1:T(2,128)} %param.7) | copy-start | bytes 12292
  184.4 39.2 %all-to-all-start.1 = ((bf16[64,20,128]{2,1,0:T(8,128)(2,1)}), bf16[64,20,128]{2,1,0:T(8,128)(2,1)}, u32[]{:S(2)}, u32[]{:S(2)}) async-start(bf16[64,20,128]{2,1,0:T(8,128)(2,1)} %convert_element_type.61), calls=%async_computation.1 | async-start | bytes 786432 | tf_op jit(solution)/shard_map/all_to_all | solution.py:63
  200.2 66.6 %all-gather.2.cloned.1.call-start = ((), (), s32[]{:S(2)}) async-start(), calls=%async_computation.4 | async-start | bytes 2359296 | tf_op jit(solution)/shard_map/all_gather | solution.py:42
  231.1 292.5 %all-reduce.3.cloned.1.call-start = ((), (), s32[]{:S(2)}) async-start(), calls=%async_computation.5 | async-start | bytes 4194304 | tf_op jit(solution)/shard_map/psum | solution.py:21
  446.4 1.0 copy-start.3
  450.0 165.3 %all-reduce.5.cloned.1.call-start = ((), (), s32[]{:S(2)}) async-start(), calls=%async_computation.6 | async-start | bytes 4194304 | tf_op jit(solution)/shard_map/psum | solution.py:21
  523.6 4.2 copy-start.1
  530.8 1.0 copy-start.4
  534.3 80.9 %copy-start.5 = (bf16[1024,512]{1,0:T(8,128)(2,1)S(1)}, bf16[1024,512]{1,0:T(8,128)(2,1)}, u32[]{:S(2)}) copy-start(bf16[1024,512]{1,0:T(8,128)(2,1)} %copy-done.4) | copy-start | bytes 3145732
Sparse Core Ops, SparseCore 0:
  147.2 35.1 reduce-scatter.3
  231.2 35.5 all-gather.1
  450.1 73.4 all-reduce.2
  534.5 80.7 all-reduce.4
where the time goes:
time: 627 us; the launch traced here: 626 us
  blocking collectives  254 us (41%)
  waiting for transfers between devices  248 us (40%)
  local copies, waits for them, and re-layouts  47.8 us (8%)
  other arithmetic  24.9 us (4%)
  matrix products  19.6 us (3%)
  starting transfers between devices  16.4 us (3%)
  between operations  14.7 us (2%)
    all_to_all x1, blocking collectives, per_device(): lax.all_to_all(send_scaled, 'expert', split_axis=0, concat_axis=0, tiled=...  160 us
    psum x2, waiting for transfers between devices, gram_sum(): return lax.psum(partial_gram.astype(jnp.bfloat16), 'dp').astype(jnp.float32)  154 us
    all_to_all x1, blocking collectives, per_device(): lax.all_to_all(send_grad, 'expert', split_axis=0, concat_axis=0, tiled=True)  94.8 us
    all_gather x1, waiting for transfers between devices, per_device(): whole_scaled = lax.all_gather(scaled_part, 'dp', axis=2, tiled=True)  35.5 us
    unnamed x5, waiting for transfers between devices  35.4 us
    all_to_all x1, waiting for transfers between devices, per_device(): lax.all_to_all(summed.reshape(experts, capacity, -1).astype(jnp.bfloat16)...  23.1 us
    scatter x2, local copies, waits for them, and re-layouts, place_slots(): return empty_rows.at[slot_index].set(values)  20.6 us
    another operation x3, other arithmetic  18.2 us
  transfers between devices with their start and end apart: 5, of which 5 were waited for; matrix products, arithmetic and copies ran while one was open for 0% of the time, Pallas kernels for 0%

commit v1 on v0

--- a/solution.py
+++ b/solution.py
@@ -2,6 +2,7 @@
 import jax.numpy as jnp
 from jax import lax
 from jax.sharding import PartitionSpec as P
+from jax.lax import all_gather
 
 D = 4096
 
@@ -18,7 +19,7 @@
 
 def gram_sum(matrix_part):
     partial_gram = jnp.dot(matrix_part, matrix_part.T, preferred_element_type=jnp.float32)
-    return lax.psum(partial_gram.astype(jnp.bfloat16), "dp").astype(jnp.float32)
+    return jnp.sum(all_gather(partial_gram.astype(jnp.bfloat16), "dp"), axis=0).astype(jnp.float32)
 
 
 def place_slots(slot_index, values, slot_count):

time: 627 us -> 664 us (1.059)
  the two profiles are of different devices: /device:TPU:2 before, /device:TPU:1 now
where the time goes in v1:
time: 664 us; the launch traced here: 663 us
  waiting for transfers between devices  284 us (43%)
  blocking collectives  246 us (37%)
  local copies, waits for them, and re-layouts  44.6 us (7%)
  other arithmetic  41.1 us (6%)
  matrix products  18.1 us (3%)
  starting transfers between devices  14.9 us (2%)
  between operations  14.7 us (2%)
    all_gather x2, waiting for transfers between devices, gram_sum(): all_gather(partial_gram.astype(jnp.bfloat16), 'dp')  182 us
    all_to_all x1, blocking collectives, per_device(): lax.all_to_all(send_scaled, 'expert', split_axis=0, concat_axis=0, tiled=...  156 us
    all_to_all x1, blocking collectives, per_device(): lax.all_to_all(send_grad, 'expert', split_axis=0, concat_axis=0, tiled=True)  89.4 us
    all_gather x1, waiting for transfers between devices, per_device(): whole_scaled = lax.all_gather(scaled_part, 'dp', axis=2, tiled=True)  41.5 us
    unnamed x5, waiting for transfers between devices  39.7 us
    all_to_all x1, waiting for transfers between devices, per_device(): lax.all_to_all(summed.reshape(experts, capacity, -1).astype(jnp.bfloat16)...  20.8 us
    scatter x2, local copies, waits for them, and re-layouts, place_slots(): return empty_rows.at[slot_index].set(values)  20.6 us
    reduce_sum x2, other arithmetic, gram_sum(): jnp.sum(all_gather(partial_gram.astype(jnp.bfloat16), 'dp'), axis=0)  18.9 us
  transfers between devices with their start and end apart: 5, of which 5 were waited for; matrix products, arithmetic and copies ran while one was open for 0% of the time, Pallas kernels for 0%

profile of v1, /device:TPU:1, one launch (start us, length us, event | category | flops | bytes accessed | tf_op | source)
XLA Modules:
  0.0 662.8 jit_solution(16515001811692064993)
XLA Ops:
  7.2 0.0 copy-start
  7.2 0.0 reduce-scatter.4.cloned.1.call-start
  7.2 0.8 broadcast_multiply_fusion
  8.0 0.8 copy.27
  8.8 0.2 eq.29
  9.0 0.2 eq.25
  9.2 0.1 copy.26
  9.3 0.2 mul.64
  9.6 18.0 %reduce-window.6 = s32[64,8,128]{2,1,0:T(8,128)S(1)} reduce-window(s32[64,8,128]{2,1,0:T(8,128)S(1)} %fusion.21, s32[]{:T(128)} %constant.33.clone.1), window={size=1x1x128 pad=0_0x0_0x127_0}, to_apply=%region_0.0 | reduce-window | flops 8323072 | bytes 524292 | tf_op jit(solution)/shard_map/reduce-window
  27.6 0.1 slice.12
  27.7 0.1 copy.29
  27.9 0.1 copy.30
  28.0 0.1 broadcast_add_fusion
  28.1 0.1 fusion.20
  28.2 12.8 %scatter_custom_fusion = bf16[1280,512]{1,0:T(8,128)(2,1)S(1)} fusion(s32[1024]{0:T(1024)S(1)} %bitcast.50, bf16[512,512]{1,0:T(8,128)(2,1)} %param.5, s32[1024]{0:T(1024)S(1)} %broadcast_clamp_fusion.1, bf16[]{:T(256)} %constant.16.clone.1), kind=kCustom, calls=%fused_computation.22 | custom fusion | bytes 1311232 | tf_op jit(solution)/shard_map/scatter | solution.py:27
  41.0 1.3 reshape.124
  42.3 89.4 %all_to_all.15 = bf16[64,20,512]{2,1,0:T(8,128)(2,1)S(1)} all-to-all(bf16[64,20,512]{2,1,0:T(8,128)(2,1)} %reshape.124), channel_id=1, replica_groups=mesh['dp'=8,'expert'=64] {'expert'}, dimensions={0} | all-to-all | bytes 2621440 | tf_op jit(solution)/shard_map/all_to_all | solution.py:48
  131.7 1.2 reshape.125
  132.9 0.0 copy-done
  132.9 4.4 convolution_convert_fusion
  137.3 4.4 copy.33
  141.7 0.0 copy-start.3
  141.7 0.0 reduce-scatter.4.cloned.1.call-update
  141.7 39.6 %reduce-scatter.4.cloned.1.call-done = bf16[128,1280]{1,0:T(8,128)(2,1)} async-done(((bf16[1024,1280]{1,0:T(8,128)(2,1)}), bf16[128,1280]{1,0:T(8,128)(2,1)}) %reduce-scatter.4.cloned.1.call-update) | async-done | bytes 327696
  181.3 1.2 copy.34
  182.5 0.8 convert_element_type.65
  183.3 14.3 %all-to-all-start.1 = ((bf16[64,20,128]{2,1,0:T(8,128)(2,1)}), bf16[64,20,128]{2,1,0:T(8,128)(2,1)S(1)}, u32[]{:S(2)}, u32[]{:S(2)}) async-start(bf16[64,20,128]{2,1,0:T(8,128)(2,1)} %convert_element_type.65), calls=%async_computation.1 | async-start | bytes 786432 | tf_op jit(solution)/shard_map/all_to_all | solution.py:64
  197.6 0.0 all-gather.6.cloned.1.call-start
  197.7 0.0 copy-done.3
  197.7 0.1 copy.25
  197.8 20.8 %all-to-all-done.1 = bf16[64,20,128]{2,1,0:T(8,128)(2,1)S(1)} async-done(((bf16[64,20,128]{2,1,0:T(8,128)(2,1)}), bf16[64,20,128]{2,1,0:T(8,128)(2,1)S(1)}, u32[]{:S(2)}, u32[]{:S(2)}) %all-to-all-start.1) | async-done | bytes 327712 | tf_op jit(solution)/shard_map/all_to_all | solution.py:64
  218.6 0.1 reshape.131
  218.7 0.0 copy-start.2
  218.7 2.8 gather_fusion
  221.5 0.0 copy-done.2
  221.5 1.4 multiply_convert_fusion.2
  222.9 0.0 all-gather.6.cloned.1.call-update
  223.0 0.2 all-gather.8.cloned.1.call-start
  223.2 41.5 %all-gather.6.cloned.1.call-done = bf16[512,2,1024]{2,1,0:T(2,128)(2,1)} async-done(((bf16[512,2,128]{2,1,0:T(2,128)(2,1)}), bf16[512,2,1024]{2,1,0:T(2,128)(2,1)}) %all-gather.6.cloned.1.call-update) | async-done | bytes 2097168 | tf_op jit(solution)/shard_map/all_gather | solution.py:43
  264.7 4.1 reshape.160
  268.8 7.8 %scatter_custom_fusion.1 = bf16[1280,1024]{1,0:T(8,128)(2,1)} fusion(s32[1024]{0:T(1024)S(1)} %bitcast.52, bf16[1024,1024]{1,0:T(8,128)(2,1)} %reshape.160, bf16[]{:T(256)} %constant.16.clone.1), kind=kCustom, calls=%fused_computation.19 | custom fusion | bytes 2621952 | tf_op jit(solution)/shard_map/scatter | solution.py:27
  276.6 5.2 reshape.129
  281.8 156.4 %all_to_all.16 = bf16[64,20,1024]{2,1,0:T(8,128)(2,1)S(1)} all-to-all(bf16[64,20,1024]{2,1,0:T(8,128)(2,1)} %reshape.129), channel_id=1, replica_groups=mesh['dp'=8,'expert'=64] {'expert'}, dimensions={0} | all-to-all | bytes 5242880 | tf_op jit(solution)/shard_map/all_to_all | solution.py:49
  438.2 2.9 bitcast_convert_fusion
  441.1 2.6 convolution_convert_fusion.2
  443.7 0.0 all-gather.8.cloned.1.call-update
  443.7 0.3 all-gather.10.cloned.1.call-start
  444.0 88.2 %all-gather.8.cloned.1.call-done = bf16[8192,1024]{1,0:T(8,128)(2,1)} async-done(((bf16[1024,1024]{1,0:T(8,128)(2,1)}), bf16[8192,1024]{1,0:T(8,128)(2,1)}) %all-gather.8.cloned.1.call-update) | async-done | bytes 16777232 | tf_op jit(solution)/shard_map/all_gather | solution.py:22
  532.2 9.5 %reduce_sum.46 = bf16[1024,1024]{1,0:T(8,128)(2,1)S(1)} reduce(bf16[8,1024,1024]{2,1,0:T(8,128)(2,1)} %bitcast.42, bf16[]{:T(256)} %constant.16.clone.1), dimensions={0}, to_apply=%region_6.7 | reduce | flops 7340032 | bytes 18874370 | tf_op jit(solution)/shard_map/reduce_sum | solution.py:22
  541.7 1.7 fusion
  544.1 1.4 subtract_convert_fusion
  545.5 0.0 copy-start.4
  545.5 1.0 copy-done.4
  546.5 2.6 convolution_convert_fusion.1
  549.1 0.0 all-gather.10.cloned.1.call-update
  549.1 93.5 %all-gather.10.cloned.1.call-done = bf16[8192,1024]{1,0:T(8,128)(2,1)} async-done(((bf16[1024,1024]{1,0:T(8,128)(2,1)}), bf16[8192,1024]{1,0:T(8,128)(2,1)}) %all-gather.10.cloned.1.call-update) | async-done | bytes 16777232 | tf_op jit(solution)/shard_map/all_gather | solution.py:22
  642.6 9.5 %reduce_sum.48 = bf16[1024,1024]{1,0:T(8,128)(2,1)S(1)} reduce(bf16[8,1024,1024]{2,1,0:T(8,128)(2,1)} %bitcast.43, bf16[]{:T(256)} %constant.16.clone.1), dimensions={0}, to_apply=%region_8.9 | reduce | flops 7340032 | bytes 18874370 | tf_op jit(solution)/shard_map/reduce_sum | solution.py:22
  652.0 0.0 copy-start.1
  652.0 4.2 multiply_bitcast_fusion
  656.3 0.0 copy-done.1
  (7 shorter events, 0.1 us)
Async XLA Ops:
  7.2 125.7 %copy-start = (bf16[1,1024,512]{2,1,0:T(8,128)(2,1)S(1)}, bf16[1,1024,512]{2,1,0:T(8,128)(2,1)}, u32[]{:S(2)}) copy-start(bf16[1,1024,512]{2,1,0:T(8,128)(2,1)} %param.9) | copy-start | bytes 3145732
  7.2 174.1 %reduce-scatter.4.cloned.1.call-start = ((), (), s32[]{:S(2)}) async-start(), calls=%async_computation.7 | async-start | bytes 2949120
  141.7 56.0 %copy-start.3 = (f32[512,2]{0,1:T(2,128)S(1)}, f32[512,2]{0,1:T(2,128)}, u32[]{:S(2)}) copy-start(f32[512,2]{0,1:T(2,128)} %param.7) | copy-start | bytes 12292
  183.3 35.3 %all-to-all-start.1 = ((bf16[64,20,128]{2,1,0:T(8,128)(2,1)}), bf16[64,20,128]{2,1,0:T(8,128)(2,1)S(1)}, u32[]{:S(2)}, u32[]{:S(2)}) async-start(bf16[64,20,128]{2,1,0:T(8,128)(2,1)} %convert_element_type.65), calls=%async_computation.1 | async-start | bytes 786432 | tf_op jit(solution)/shard_map/all_to_all | solution.py:64
  197.6 67.1 %all-gather.6.cloned.1.call-start = ((), (), s32[]{:S(2)}) async-start(), calls=%async_computation.4 | async-start | bytes 2359296 | tf_op jit(solution)/shard_map/all_gather | solution.py:43
  218.7 2.8 copy-start.2
  223.0 309.3 %all-gather.8.cloned.1.call-start = ((), (), s32[]{:S(2)}) async-start(), calls=%async_computation.5 | async-start | bytes 18874368 | tf_op jit(solution)/shard_map/all_gather | solution.py:22
  443.7 198.9 %all-gather.10.cloned.1.call-start = ((), (), s32[]{:S(2)}) async-start(), calls=%async_computation.6 | async-start | bytes 18874368 | tf_op jit(solution)/shard_map/all_gather | solution.py:22
  545.5 1.0 copy-start.4
  652.0 4.3 copy-start.1
Sparse Core Ops, SparseCore 0:
  141.8 39.4 reduce-scatter.3
  223.1 41.6 all-gather.5
  443.8 88.3 all-gather.7
  549.2 93.2 all-gather.9
